TPU v7x, 32 devices: a whole 2x2x4 slice. The times are simulated.
32 devices in a mesh: pair: 2 (over core), shot: 16 (over z, y, x).
Axes of the slice: x: 2, y: 2, z: 4, core: 2. Of those that a mesh axis runs over, the one named last changes fastest.
Arguments:
- records: bfloat16 [4, 384, 384, 128], P('pair', 'shot'), may hold values from -6 to 6
- surface: float32 [16, 384], P('shot'), may hold values from 0.4 to 1.2
- mirror: int32 [4], replicated, may hold values from 0 to 3, as said below
Outputs:
- predicted: bfloat16 [4, 384, 384, 128], P('pair', 'shot')
Inputs may be any that keep to these rules, and one draw needn't show every extreme that they name: mirror is an involution without fixed points: mirror[mirror[g]] = g and mirror[g] differs from g for every group.
All inputs are finite; a program needn't handle non-finite values.
Results may differ from a plain program's by a relative error of at most 0.0088.
Values may be sent and summed in bfloat16 or wider, within the bound.
A program may use at most 128 MiB of HBM per device.

v0:
```python
import math

import jax
import jax.numpy as jnp
from jax import lax
from jax.sharding import PartitionSpec as P

ORDERS = 2


def make_tables(freqs, time):
    product = (
        jnp.arange(1, freqs + 1, dtype=jnp.int32)[:, None]
        * jnp.arange(time, dtype=jnp.int32)[None, :]
        % time
    )
    phase = product.astype(jnp.float32) * (2.0 * math.pi / time)
    cosine = jnp.cos(phase)
    sine = jnp.sin(phase)
    forward = (jnp.stack([cosine, -sine], axis=1) * math.sqrt(2.0 / time)).astype(jnp.bfloat16)
    inverse = (jnp.stack([cosine, -sine], axis=1) / math.sqrt(freqs)).astype(jnp.bfloat16)
    return (forward, inverse)


def batch_dot(left, right):
    return jnp.einsum("kij,kjl->kil", left, right, preferred_element_type=jnp.float32)


def chain_products(own_spec, mate_spec, scale):
    mate_re = mate_spec[:, 0]
    mate_im = mate_spec[:, 1]
    width = mate_spec.shape[-1]
    column_scale = scale[:, None, None, :]
    block = jnp.concatenate(
        [jnp.concatenate([mate_re, mate_im], axis=2), jnp.concatenate([-mate_im, mate_re], axis=2)],
        axis=1,
    )
    left = (own_spec.astype(jnp.float32) * column_scale).astype(jnp.bfloat16)
    total = jnp.zeros(own_spec.shape, jnp.float32)
    for order_index in range(ORDERS):
        wide_left = jnp.concatenate([left[:, 0], left[:, 1]], axis=2)
        joined = batch_dot(wide_left, block)
        product = jnp.stack([joined[..., :width], joined[..., width:]], axis=1)
        total = total + product
        if order_index + 1 < ORDERS:
            left = (product * column_scale).astype(jnp.bfloat16)
    return total.astype(jnp.bfloat16)


def local(records, surface, mirror):
    shot_count = lax.axis_size("shot")
    freqs = surface.shape[0] * shot_count
    time = records.shape[-1]
    receivers = records.shape[2]
    local_groups = records.shape[0]
    forward, inverse = make_tables(freqs, time)
    spectra = jnp.einsum(
        "kct,gsrt->gkcsr", forward, records, preferred_element_type=jnp.float32
    ).astype(jnp.bfloat16)
    first_group = lax.axis_index("pair") * local_groups
    target = lax.dynamic_slice_in_dim(mirror, first_group, local_groups, 0)
    own_spec = lax.all_to_all(spectra, "shot", split_axis=1, concat_axis=3, tiled=True)
    piece = lax.all_gather(own_spec, "pair", axis=0, tiled=True)
    index = jnp.arange(piece.shape[0], dtype=jnp.int32)
    onehot = (target[:, None] == index[None, :]).astype(jnp.bfloat16)
    flat = piece.reshape((piece.shape[0], -1))
    chosen = jnp.dot(onehot, flat, preferred_element_type=jnp.float32)
    mate_spec = chosen.astype(jnp.bfloat16).reshape(jnp.zeros_like(own_spec).shape)
    scale = -surface / math.sqrt(2.0 * receivers)
    merged_shape = (-1,) + own_spec.shape[2:]
    total = chain_products(
        own_spec.reshape(merged_shape),
        mate_spec.reshape(merged_shape),
        jnp.tile(scale, (local_groups, 1)),
    )
    total = total.reshape(own_spec.shape)
    return jnp.einsum(
        "gkcsr,kct->gsrt",
        lax.all_to_all(total, "shot", split_axis=3, concat_axis=1, tiled=True),
        inverse,
        preferred_element_type=jnp.float32,
    ).astype(jnp.bfloat16)


def solution(mesh):
    return jax.shard_map(
        local,
        mesh=mesh,
        in_specs=(P("pair", "shot", None, None), P("shot", None), P()),
        out_specs=P("pair", "shot", None, None),
        check_vma=False,
    )
```

profile of v0, /device:TPU:0, one launch (start us, length us, event | category | flops | bytes accessed | tf_op | source)
XLA Modules:
  0.0 116.2 jit_solution(5050923782856392728)
XLA Ops:
  6.5 0.0 all-gather.2.cloned.1.call-start
  6.5 0.1 fusion.33
  6.7 4.0 %fusion.8 = bf16[2,16,2,24,384]{4,1,3,0,2:T(8,128)(2,1)S(1)} fusion(bf16[2,24,384,128]{3,2,1,0:T(8,128)(2,1)} %param.3, f32[16,1,128]{2,0,1:T(8,128)S(1)} %get-tuple-element.18, f32[16,1,128]{2,0,1:T(8,128)S(1)} %get-tuple-element.17), kind=kOutput, calls=%fused_computation.12 | convolution fusion | flops 151597056 | bytes 5914624 | tf_op jit(solution)/shard_map/kct,gsrt->gkcsr/dot_general | solution.py:57
  10.7 0.3 copy.20
  11.0 38.1 %all_to_all.36 = bf16[2,16,2,24,384]{4,3,0,2,1:T(8,128)(2,1)S(1)} all-to-all(bf16[2,16,2,24,384]{4,3,0,2,1:T(8,128)(2,1)S(1)} %copy.20), channel_id=1, replica_groups=mesh['pair'=2,'shot'=16] {'shot'}, dimensions={1} | all-to-all | bytes 2359296 | tf_op jit(solution)/shard_map/all_to_all | solution.py:62
  49.1 0.0 copy-start.1
  49.1 0.0 copy-start
  49.1 1.1 copy.21
  50.2 0.0 all-gather.2.cloned.1.call-update
  50.3 0.0 copy-done.1
  50.3 0.1 dynamic_slice.3
  50.4 0.0 copy-done
  50.4 1.5 %fusion.4 = bf16[2,2,384,384]{3,2,0,1:T(8,128)(2,1)S(1)} fusion(f32[384]{0:T(512)S(1)} %multiply_reduce_fusion, bf16[2,16,2,24,384]{4,3,1,2,0:T(8,128)(2,1)} %copy.21), kind=kLoop, calls=%fused_computation.10 | loop fusion | flops 1769472 | bytes 2360832 | tf_op jit(solution)/shard_map/convert_element_type | solution.py:38
  51.9 0.1 slice_bitcast_fusion.11
  52.0 6.9 %all-gather.2.cloned.1.call-done = bf16[4,1,2,384,384]{4,3,2,1,0:T(8,128)(2,1)} async-done(((bf16[2,1,2,384,384]{4,3,2,1,0:T(8,128)(2,1)}), bf16[4,1,2,384,384]{4,3,2,1,0:T(8,128)(2,1)}) %all-gather.2.cloned.1.call-update) | async-done | bytes 2359312 | tf_op jit(solution)/shard_map/all_gather | solution.py:63
  58.9 3.5 %copy.36 = bf16[1,4,768,384]{3,1,2,0:T(4,128)(2,1)S(1)} copy(bf16[1,4,768,384]{3,2,1,0:T(8,128)(2,1)} %bitcast.81) | data formatting | bytes 4718592
  62.4 1.4 %convolution_convert_fusion = bf16[2,294912]{1,0:T(2,128)(2,1)S(1)} fusion(bf16[4,294912]{1,0:T(4,128)(2,1)S(1)} %bitcast.82, s32[2]{0:T(128)S(1)} %dynamic_slice.3), kind=kOutput, calls=%fused_computation | convolution fusion | flops 5308424 | bytes 3538952 | tf_op jit(solution)/shard_map/dot_general | solution.py:67
  63.8 0.2 copy.37
  64.0 0.1 fusion.43
  64.0 0.1 slice_bitcast_fusion.8
  64.1 1.3 %fusion.11 = f32[2,384,768]{2,1,0:T(8,128)S(1)} fusion(bf16[2,384,384]{2,1,0:T(8,128)(2,1)S(1)} %get-tuple-element.16, bf16[2,384,384]{2,1,0:T(8,128)(2,1)S(1)} %get-tuple-element.15, bf16[2,384,384]{2,1,0:T(8,128)(2,1)S(1)} %get-tuple-element.14, bf16[2,384,384]{2,1,0:T(8,128)(2,1)S(1)} %fusion.43, bf16[2,384,384]{2,1,0:T(8,128)(2,1)S(1)} %get-tuple-element.13), kind=kOutput, calls=%fused_computation.15 | convolution fusion | flops 917766144 | bytes 5308416 | tf_op jit(solution)/shard_map/kij,kjl->kil/dot_general | solution.py:26
  65.5 0.3 slice_bitcast_fusion.4
  65.8 0.2 fusion.3
  66.0 0.1 slice_bitcast_fusion.7
  66.2 1.3 %fusion.15 = f32[2,384,768]{2,1,0:T(8,128)S(1)} fusion(bf16[2,384,384]{2,1,0:T(8,128)(2,1)S(1)} %get-tuple-element.12, bf16[2,384,384]{2,1,0:T(8,128)(2,1)S(1)} %get-tuple-element.11, bf16[2,384,384]{2,1,0:T(8,128)(2,1)S(1)} %get-tuple-element.14, bf16[2,384,384]{2,1,0:T(8,128)(2,1)S(1)} %fusion.43, bf16[2,384,384]{2,1,0:T(8,128)(2,1)S(1)} %get-tuple-element.13), kind=kOutput, calls=%fused_computation.19 | convolution fusion | flops 917766144 | bytes 5308416 | tf_op jit(solution)/shard_map/kij,kjl->kil/dot_general | solution.py:26
  67.5 0.2 slice_bitcast_fusion.1
  67.6 0.4 fusion.2
  68.0 1.2 %copy.26 = bf16[2,1,2,384,384]{4,0,2,1,3:T(2,128)(2,1)S(1)} copy(bf16[2,1,2,384,384]{4,3,0,2,1:T(8,128)(2,1)S(1)} %fusion.2) | data formatting | bytes 2359296 | tf_op jit(solution)/shard_map/convert_element_type | solution.py:47
  69.2 37.0 %all_to_all.37 = bf16[2,1,2,384,384]{4,0,2,1,3:T(2,128)(2,1)S(1)} all-to-all(bf16[2,1,2,384,384]{4,0,2,1,3:T(2,128)(2,1)S(1)} %copy.26), channel_id=1, replica_groups=mesh['pair'=2,'shot'=16] {'shot'}, dimensions={3} | all-to-all | bytes 2359296 | tf_op jit(solution)/shard_map/all_to_all | solution.py:79
  106.3 3.1 %bitcast_convert_fusion = bf16[2,24,384,128]{3,2,1,0:T(8,128)(2,1)} fusion(bf16[2,1,2,16,24,384]{5,0,2,4,3,1:T(2,128)(2,1)S(1)} %bitcast.80, f32[16,1,128]{2,0,1:T(8,128)S(1)} %get-tuple-element.18, f32[16,1,128]{2,0,1:T(8,128)S(1)} %get-tuple-element.17), kind=kOutput, calls=%fused_computation.1 | convolution fusion | flops 153366528 | bytes 5914624 | tf_op jit(solution)/shard_map/gkcsr,kct->gsrt/dot_general | solution.py:77
  (2 shorter events, 0.0 us)
Async XLA Ops:
  6.5 52.3 %all-gather.2.cloned.1.call-start = ((), (), s32[]{:S(2)}) async-start(), calls=%async_computation.2 | async-start | bytes 3538944 | tf_op jit(solution)/shard_map/all_gather | solution.py:63
  49.1 1.2 %copy-start.1 = (s32[4]{0:T(128)S(1)}, s32[4]{0:T(128)}, u32[]{:S(2)}) copy-start(s32[4]{0:T(128)} %param.5) | copy-start | bytes 52
  49.1 1.3 %copy-start = (f32[1,384]{1,0:T(1,128)S(1)}, f32[1,384]{1,0:T(1,128)}, u32[]{:S(2)}) copy-start(f32[1,384]{1,0:T(1,128)} %param.4) | copy-start | bytes 4612
Sparse Core Ops, SparseCore 0:
  50.4 8.4 all-gather.1
where the time goes:
time: 116 us
  blocking collectives  75.1 us (65%)
  between operations  13.5 us (12%)
  matrix products  11.2 us (10%)
  local copies, waits for them, and re-layouts  7.16 us (6%)
  waiting for transfers between devices  6.88 us (6%)
  other arithmetic  2.31 us (2%)
    all_to_all x1, blocking collectives, local(): lax.all_to_all(spectra, 'shot', split_axis=1, concat_axis=3, tiled=True)  38.1 us
    all_to_all x1, blocking collectives, local(): lax.all_to_all(total, 'shot', split_axis=3, concat_axis=1, tiled=True)  37 us
    all_gather x1, waiting for transfers between devices, local(): piece = lax.all_gather(own_spec, 'pair', axis=0, tiled=True)  6.86 us
    dot_general x1, matrix products, local(): jnp.einsum('kct,gsrt->gkcsr', forward, records, preferred_element_type=jn...  4.04 us
    unnamed x6, local copies, waits for them, and re-layouts  3.65 us
    dot_general x1, matrix products, local(): jnp.einsum('gkcsr,kct->gsrt', lax.all_to_all(total, 'shot', split_axis=3,...  3.11 us
    dot_general x2, matrix products, batch_dot(): jnp.einsum('kij,kjl->kil', left, right, preferred_element_type=jnp.float32)  2.63 us
  transfers between devices with their start and end apart: 1, of which 1 were waited for; matrix products, arithmetic and copies ran while one was open for 1% of the time, Pallas kernels for 0%

commit v1 on v0

v1 whole, which is shorter than its diff:
```python
import functools
import math

import jax
import jax.numpy as jnp
from jax import lax
from jax.experimental import pallas as pl
from jax.experimental.pallas import tpu as pltpu
from jax.sharding import PartitionSpec as P

ORDERS = 2
MESH = pl.DeviceIdType.MESH


def make_tables(freqs, time):
    product = (
        jnp.arange(1, freqs + 1, dtype=jnp.int32)[:, None]
        * jnp.arange(time, dtype=jnp.int32)[None, :]
        % time
    )
    phase = product.astype(jnp.float32) * (2.0 * math.pi / time)
    cosine = jnp.cos(phase)
    sine = jnp.sin(phase)
    forward = (jnp.stack([cosine, -sine], axis=1) * math.sqrt(2.0 / time)).astype(jnp.bfloat16)
    inverse = (jnp.stack([cosine, -sine], axis=1) / math.sqrt(freqs)).astype(jnp.bfloat16)
    return (forward, inverse)


def kernel(
    chips, cores, target_ref, scale_ref, send_ref, out_ref,
    held, left, block, first, totals,
    own_sem, send_sems, recv_sems, pass_sems, pass_recv_sems, back_send_sems, back_recv_sems,
):
    me = lax.axis_index("shot")
    core = lax.axis_index("pair")
    groups, parts, shots, width = send_ref.shape[1:]
    freqs = parts // 2

    def chip(step):
        return lax.rem(me + step, chips)

    def back_chip(step):
        return lax.rem(me - step + chips, chips)

    def peer(step):
        return lax.rem(core + step, cores)

    def rows(index):
        return pl.ds(pl.multiple_of(index * shots, shots), shots)

    barrier = pltpu.get_barrier_semaphore()

    @pl.loop(1, chips)
    def _(step):
        pl.semaphore_signal(barrier, inc=1, device_id=(core, chip(step)), device_id_type=MESH)

    for step in range(1, cores):
        pl.semaphore_signal(barrier, inc=1, device_id=(peer(step), me), device_id_type=MESH)
    pl.semaphore_wait(barrier, chips + cores - 2)

    def spread(step):
        return pltpu.make_async_remote_copy(
            src_ref=send_ref.at[chip(step)],
            dst_ref=held.at[core, :, :, me],
            send_sem=send_sems.at[step],
            recv_sem=recv_sems.at[step],
            device_id=(core, chip(step)),
            device_id_type=MESH,
        )

    def hand_on(step, other):
        source = back_chip(step)
        return pltpu.make_async_remote_copy(
            src_ref=held.at[core, :, :, source],
            dst_ref=held.at[core, :, :, source],
            send_sem=pass_sems.at[other, step],
            recv_sem=pass_recv_sems.at[other, step],
            device_id=(peer(other), me),
            device_id_type=MESH,
        )

    @pl.loop(1, chips)
    def _(step):
        spread(step).start()

    own = pltpu.make_async_copy(send_ref.at[me], held.at[core, :, :, me], own_sem)
    own.start()
    own.wait()
    for other in range(1, cores):
        hand_on(0, other).start()

    @pl.loop(1, chips)
    def _(step):
        spread(step).wait_recv()
        for other in range(1, cores):
            hand_on(step, other).start()

    @pl.loop(0, chips)
    def _(step):
        for other in range(1, cores):
            hand_on(step, other).wait()

    def matrix(slot, group, part):
        value = held[slot, group, part].astype(jnp.float32)
        return value.reshape(chips * shots, width)

    def send_back(step, group):
        return pltpu.make_async_remote_copy(
            src_ref=totals.at[chip(step), group],
            dst_ref=out_ref.at[me, group],
            send_sem=back_send_sems.at[group, step],
            recv_sem=back_recv_sems.at[group, step],
            device_id=(core, chip(step)),
            device_id_type=MESH,
        )

    tall = chips * shots
    span = 16 if chips % 16 == 0 else chips
    tile = width if width % 256 == 0 else 2 * width
    for group in range(groups):
        mate = target_ref[group]
        mate_slot = mate // groups
        mate_group = lax.rem(mate, groups)
        for freq in range(freqs):
            scale = scale_ref[pl.ds(freq, 1), :]
            mate_re = matrix(mate_slot, mate_group, 2 * freq)
            mate_im = matrix(mate_slot, mate_group, 2 * freq + 1)
            block[:tall, :width] = mate_re.astype(jnp.bfloat16)
            block[tall:, width:] = mate_re.astype(jnp.bfloat16)
            block[:tall, width:] = mate_im.astype(jnp.bfloat16)
            block[tall:, :width] = (-mate_im).astype(jnp.bfloat16)
            for part in range(2):
                columns = slice(part * width, (part + 1) * width)
                value = matrix(core, group, 2 * freq + part)
                left[:, columns] = (value * scale).astype(jnp.bfloat16)
            for order in range(ORDERS):
                for top in range(0, chips, span):
                    band = slice(top * shots, (top + span) * shots)
                    pieces = []
                    for start in range(0, 2 * width, tile):
                        piece = jnp.dot(
                            left[band, :], block[:, start : start + tile],
                            preferred_element_type=jnp.float32,
                        )
                        if order > 0:
                            piece = piece + first[band, start : start + tile]
                        if order + 1 < ORDERS:
                            first[band, start : start + tile] = piece
                            pieces.append(piece)
                        else:
                            for low in range(start, start + tile, width):
                                total = piece[:, low - start : low - start + width]
                                totals[top : top + span, group, 2 * freq + low // width] = (
                                    total.reshape(span, shots, width).astype(jnp.bfloat16)
                                )
                    if order + 1 < ORDERS:
                        product = jnp.concatenate(pieces, axis=1) if len(pieces) > 1 else pieces[0]
                        wide = jnp.concatenate([scale, scale], axis=1)
                        left[band, :] = (product * wide).astype(jnp.bfloat16)

        @pl.loop(1, chips)
        def _(step):
            send_back(step, group).start()

        out_ref[me, group] = totals[me, group]

    @pl.loop(1, chips)
    def _(step):
        spread(step).wait_send()
        for group in range(groups):
            send_back(step, group).wait()


def local(records, surface, mirror):
    chips = lax.axis_size("shot")
    cores = lax.axis_size("pair")
    groups, shots, receivers, time = records.shape
    freqs = surface.shape[0]
    forward, inverse = make_tables(freqs * chips, time)
    spectra = jnp.einsum(
        "kct,gsrt->kgcsr", forward, records, preferred_element_type=jnp.float32
    ).astype(jnp.bfloat16)
    spectra = spectra.reshape(chips, freqs, groups, 2, shots, receivers)
    spectra = spectra.swapaxes(1, 2).reshape(chips, groups, 2 * freqs, shots, receivers)
    first_group = lax.axis_index("pair") * groups
    target = lax.dynamic_slice_in_dim(mirror, first_group, groups, 0)
    scale = -surface / math.sqrt(2.0 * receivers)
    tall = chips * shots
    block_shape = (chips, groups, 2 * freqs, shots, receivers)
    dma = pltpu.SemaphoreType.DMA
    total = pl.pallas_call(
        functools.partial(kernel, chips, cores),
        out_shape=jax.ShapeDtypeStruct(block_shape, jnp.bfloat16),
        in_specs=[
            pl.BlockSpec(memory_space=pltpu.SMEM),
            pl.BlockSpec(memory_space=pltpu.VMEM),
            pl.BlockSpec(memory_space=pltpu.VMEM),
        ],
        out_specs=pl.BlockSpec(memory_space=pltpu.VMEM),
        scratch_shapes=[
            pltpu.VMEM((cores, groups, 2 * freqs, chips, shots, receivers), jnp.bfloat16),
            pltpu.VMEM((tall, 2 * receivers), jnp.bfloat16),
            pltpu.VMEM((2 * tall, 2 * receivers), jnp.bfloat16),
            pltpu.VMEM((tall, 2 * receivers), jnp.float32),
            pltpu.VMEM(block_shape, jnp.bfloat16),
            dma,
            dma((chips,)),
            dma((chips,)),
            dma((cores, chips)),
            dma((cores, chips)),
            dma((groups, chips)),
            dma((groups, chips)),
        ],
        compiler_params=pltpu.CompilerParams(
            collective_id=0, has_side_effects=True, vmem_limit_bytes=60 * 1024 * 1024
        ),
    )(target, scale, spectra)
    total = total.reshape(chips, groups, freqs, 2, shots, receivers)
    table = inverse.reshape(chips, freqs, 2, time)
    return jnp.einsum(
        "ngfcsr,nfct->gsrt", total, table, preferred_element_type=jnp.float32
    ).astype(jnp.bfloat16)


def solution(mesh):
    return jax.shard_map(
        local,
        mesh=mesh,
        in_specs=(P("pair", "shot", None, None), P("shot", None), P()),
        out_specs=P("pair", "shot", None, None),
        check_vma=False,
    )
```

time: 116 us -> 79.8 us (0.69)
  the two profiles are of different devices: /device:TPU:0 before, /device:TPU:20 now
where the time goes in v1:
time: 79.8 us; the launch traced here: 79.6 us
  Pallas kernels  66.7 us (84%)
  matrix products  8.95 us (11%)
  local copies, waits for them, and re-layouts  2.54 us (3%)
  other arithmetic  1.38 us (2%)
    pallas_call x1, Pallas kernels, local(): pl.pallas_call(functools.partial(kernel, chips, cores), out_shape=jax.Sha...  66.7 us
    dot_general x1, matrix products, local(): jnp.einsum('ngfcsr,nfct->gsrt', total, table, preferred_element_type=jnp....  4.91 us
    dot_general x1, matrix products, local(): jnp.einsum('kct,gsrt->kgcsr', forward, records, preferred_element_type=jn...  4.04 us

profile of v1, /device:TPU:20, one launch (start us, length us, event | category | flops | bytes accessed | tf_op | source)
XLA Modules:
  0.0 79.6 jit_solution(10235220040404940428)
XLA Ops:
  0.0 1.3 %dynamic_slice.3.target_ref = s32[2]{0:T(128)} dynamic-slice(s32[4]{0:T(128)} %param.5, s32[]{:T(128)S(6)} %select_n.23), dynamic_slice_sizes={2} | dynamic-slice | bytes 20 | tf_op jit(solution)/shard_map/dynamic_slice | solution.py:186
  1.3 1.2 %negate_multiply_fusion.scale_ref = f32[1,384]{1,0:T(1,128)} fusion(f32[1,384]{1,0:T(1,128)} %param.4), kind=kLoop, calls=%fused_computation.24 | loop fusion | flops 768 | bytes 3072 | tf_op jit(solution)/shard_map/div | solution.py:187
  2.5 0.1 fusion.16
  2.6 4.0 %fusion = bf16[16,2,2,24,384]{4,0,3,2,1:T(8,128)(2,1)S(1)} fusion(bf16[2,24,384,128]{3,2,1,0:T(8,128)(2,1)} %param.3, f32[16,1,128]{2,0,1:T(8,128)S(1)} %get-tuple-element.6, f32[16,1,128]{2,0,1:T(8,128)S(1)} %get-tuple-element.5), kind=kOutput, calls=%fused_computation.1 | convolution fusion | flops 151007232 | bytes 5914624 | tf_op jit(solution)/shard_map/kct,gsrt->kgcsr/dot_general | solution.py:180
  6.7 1.3 %copy.14 = bf16[16,2,2,24,384]{4,3,1,2,0:T(8,128)(2,1)} copy(bf16[16,2,2,24,384]{4,0,3,2,1:T(8,128)(2,1)S(1)} %fusion) | data formatting | bytes 2359296 | tf_op jit(solution)/shard_map/kct,gsrt->kgcsr/dot_general | solution.py:180
  8.0 66.7 %shard_map.37 = bf16[16,2,2,24,384]{4,3,2,1,0:T(8,128)(2,1)} custom-call(s32[2]{0:T(128)} %dynamic_slice.3.target_ref, f32[1,384]{1,0:T(1,128)} %negate_multiply_fusion.scale_ref, bf16[16,2,2,24,384]{4,3,2,1,0:T(8,128)(2,1)} %bitcast.19), custom_call_target="tpu_custom_call" | custom-call | tf_op jit(solution)/shard_map/pallas_call | solution.py:191
  74.6 4.9 %bitcast_convert_fusion = bf16[2,24,384,128]{3,2,1,0:T(8,128)(2,1)} fusion(bf16[16,2,2,24,384]{4,3,2,1,0:T(8,128)(2,1)} %shard_map.37, f32[16,1,128]{2,0,1:T(8,128)S(1)} %get-tuple-element.6, f32[16,1,128]{2,0,1:T(8,128)S(1)} %get-tuple-element.5), kind=kOutput, calls=%fused_computation | convolution fusion | flops 153366528 | bytes 5914624 | tf_op jit(solution)/shard_map/ngfcsr,nfct->gsrt/dot_general | solution.py:220
  (1 shorter events, 0.0 us)

commit v2 on v1

v2 whole, which is shorter than its diff:
```python
import functools
import math

import jax
import jax.numpy as jnp
from jax import lax
from jax.experimental import pallas as pl
from jax.experimental.pallas import tpu as pltpu
from jax.sharding import PartitionSpec as P

ORDERS = 2
MESH = pl.DeviceIdType.MESH


def make_tables(freqs, time):
    product = (
        jnp.arange(1, freqs + 1, dtype=jnp.int32)[:, None]
        * jnp.arange(time, dtype=jnp.int32)[None, :]
        % time
    )
    phase = product.astype(jnp.float32) * (2.0 * math.pi / time)
    cosine = jnp.cos(phase)
    sine = jnp.sin(phase)
    forward = (jnp.stack([cosine, -sine], axis=1) * math.sqrt(2.0 / time)).astype(jnp.bfloat16)
    inverse = (jnp.stack([cosine, -sine], axis=1) / math.sqrt(freqs)).astype(jnp.bfloat16)
    return (forward, inverse)


def kernel(
    chips, cores, mirror_ref, surface_ref, forward_ref, records_ref, out_ref,
    traces, stage, send, held, left, block, first, totals, back,
    load_sems, own_sems, send_sems, recv_sems, pass_sems, pass_recv_sems, back_send_sems, back_recv_sems,
):
    me = lax.axis_index("shot")
    core = lax.axis_index("pair")
    groups, parts, shots, width = send.shape[1:]
    freqs = parts // 2
    loads = load_sems.shape[1]
    chunk = shots // loads

    def chip(step):
        return lax.rem(me + step, chips)

    def back_chip(step):
        return lax.rem(me - step + chips, chips)

    def peer(step):
        return lax.rem(core + step, cores)

    def far_first(index):
        turned = index + chips // 2 - 1
        return jnp.where(turned >= chips, turned - chips + 1, turned)

    def load(group, index):
        some = pl.ds(index * chunk, chunk)
        return pltpu.make_async_copy(
            records_ref.at[group, some], traces.at[group, some], load_sems.at[group, index]
        )

    for group in range(groups):
        for index in range(loads):
            load(group, index).start()

    barrier = pltpu.get_barrier_semaphore()

    @pl.loop(1, chips)
    def _(step):
        pl.semaphore_signal(barrier, inc=1, device_id=(core, chip(step)), device_id_type=MESH)

    for step in range(1, cores):
        pl.semaphore_signal(barrier, inc=1, device_id=(peer(step), me), device_id_type=MESH)

    def spread(step, group):
        return pltpu.make_async_remote_copy(
            src_ref=send.at[chip(step), group],
            dst_ref=held.at[core, group, :, me],
            send_sem=send_sems.at[group, step],
            recv_sem=recv_sems.at[group, step],
            device_id=(core, chip(step)),
            device_id_type=MESH,
        )

    def hand_on(step, other, group):
        source = back_chip(step)
        return pltpu.make_async_remote_copy(
            src_ref=held.at[core, group, :, source],
            dst_ref=held.at[core, group, :, source],
            send_sem=pass_sems.at[other, group, step],
            recv_sem=pass_recv_sems.at[other, group, step],
            device_id=(peer(other), me),
            device_id_type=MESH,
        )

    def keep(group):
        return pltpu.make_async_copy(
            send.at[me, group], held.at[core, group, :, me], own_sems.at[group]
        )

    def send_back(step, group):
        return pltpu.make_async_remote_copy(
            src_ref=totals.at[chip(step), group],
            dst_ref=back.at[me, group],
            send_sem=back_send_sems.at[group, step],
            recv_sem=back_recv_sems.at[group, step],
            device_id=(core, chip(step)),
            device_id_type=MESH,
        )

    for group in range(groups):
        for index in range(loads):
            load(group, index).wait()
            for shot in range(index * chunk, (index + 1) * chunk):
                stage[shot] = lax.dot_general(
                    forward_ref[...], traces[group, shot], (((1,), (1,)), ((), ())),
                    preferred_element_type=jnp.float32,
                )
        for row in range(chips * parts):
            send[row // parts, group, row % parts] = stage[:, row, :].astype(jnp.bfloat16)
        if group == 0:
            pl.semaphore_wait(barrier, chips + cores - 2)

        @pl.loop(1, chips)
        def _(index):
            spread(far_first(index), group).start()

        keep(group).start()

    for group in range(groups):
        keep(group).wait()
        for other in range(1, cores):
            hand_on(0, other, group).start()

        @pl.loop(1, chips)
        def _(index):
            step = far_first(index)
            spread(step, group).wait_recv()
            for other in range(1, cores):
                hand_on(step, other, group).start()

    @pl.loop(0, chips)
    def _(step):
        for group in range(groups):
            for other in range(1, cores):
                hand_on(step, other, group).wait()

    def matrix(slot, group, part):
        value = held[slot, group, part].astype(jnp.float32)
        return value.reshape(chips * shots, width)

    tall = chips * shots
    span = 16 if chips % 16 == 0 else chips
    tile = width if width % 256 == 0 else 2 * width
    for group in range(groups):
        mate = mirror_ref[core * groups + group]
        mate_slot = mate // groups
        mate_group = lax.rem(mate, groups)
        for freq in range(freqs):
            scale = -surface_ref[pl.ds(freq, 1), :] / math.sqrt(2.0 * width)
            mate_re = matrix(mate_slot, mate_group, 2 * freq)
            mate_im = matrix(mate_slot, mate_group, 2 * freq + 1)
            block[:tall, :width] = mate_re.astype(jnp.bfloat16)
            block[tall:, width:] = mate_re.astype(jnp.bfloat16)
            block[:tall, width:] = mate_im.astype(jnp.bfloat16)
            block[tall:, :width] = (-mate_im).astype(jnp.bfloat16)
            for part in range(2):
                columns = slice(part * width, (part + 1) * width)
                value = matrix(core, group, 2 * freq + part)
                left[:, columns] = (value * scale).astype(jnp.bfloat16)
            for order in range(ORDERS):
                for top in range(0, chips, span):
                    band = slice(top * shots, (top + span) * shots)
                    pieces = []
                    for start in range(0, 2 * width, tile):
                        piece = jnp.dot(
                            left[band, :], block[:, start : start + tile],
                            preferred_element_type=jnp.float32,
                        )
                        if order > 0:
                            piece = piece + first[band, start : start + tile]
                        if order + 1 < ORDERS:
                            first[band, start : start + tile] = piece
                            pieces.append(piece)
                        else:
                            for low in range(start, start + tile, width):
                                total = piece[:, low - start : low - start + width]
                                totals[top : top + span, group, 2 * freq + low // width] = (
                                    total.reshape(span, shots, width).astype(jnp.bfloat16)
                                )
                    if order + 1 < ORDERS:
                        product = jnp.concatenate(pieces, axis=1) if len(pieces) > 1 else pieces[0]
                        wide = jnp.concatenate([scale, scale], axis=1)
                        left[band, :] = (product * wide).astype(jnp.bfloat16)

        @pl.loop(1, chips)
        def _(index):
            send_back(far_first(index), group).start()

        back[me, group] = totals[me, group]

    @pl.loop(1, chips)
    def _(step):
        for group in range(groups):
            spread(step, group).wait_send()

    for group in range(groups):

        @pl.loop(1, chips)
        def _(index):
            send_back(far_first(index), group).wait()

        for row in range(chips * parts):
            stage[:, row, :] = back[row // parts, group, row % parts].astype(jnp.float32)
        out_ref[group] = stage[...].astype(jnp.bfloat16)


def local(records, surface, mirror):
    chips = lax.axis_size("shot")
    cores = lax.axis_size("pair")
    groups, shots, receivers, time = records.shape
    freqs = surface.shape[0]
    parts = 2 * freqs
    forward, inverse = make_tables(freqs * chips, time)
    tall = chips * shots
    loads = 4 if shots % 4 == 0 else 1
    block_shape = (chips, groups, parts, shots, receivers)
    dma = pltpu.SemaphoreType.DMA
    total = pl.pallas_call(
        functools.partial(kernel, chips, cores),
        out_shape=jax.ShapeDtypeStruct((groups, shots, chips * parts, receivers), jnp.bfloat16),
        in_specs=[
            pl.BlockSpec(memory_space=pltpu.SMEM),
            pl.BlockSpec(memory_space=pltpu.VMEM),
            pl.BlockSpec(memory_space=pltpu.VMEM),
            pl.BlockSpec(memory_space=pl.ANY),
        ],
        out_specs=pl.BlockSpec(memory_space=pltpu.VMEM),
        scratch_shapes=[
            pltpu.VMEM(records.shape, jnp.bfloat16),
            pltpu.VMEM((shots, chips * parts, receivers), jnp.float32),
            pltpu.VMEM(block_shape, jnp.bfloat16),
            pltpu.VMEM((cores, groups, parts, chips, shots, receivers), jnp.bfloat16),
            pltpu.VMEM((tall, 2 * receivers), jnp.bfloat16),
            pltpu.VMEM((2 * tall, 2 * receivers), jnp.bfloat16),
            pltpu.VMEM((tall, 2 * receivers), jnp.float32),
            pltpu.VMEM(block_shape, jnp.bfloat16),
            pltpu.VMEM(block_shape, jnp.bfloat16),
            dma((groups, loads)),
            dma((groups,)),
            dma((groups, chips)),
            dma((groups, chips)),
            dma((cores, groups, chips)),
            dma((cores, groups, chips)),
            dma((groups, chips)),
            dma((groups, chips)),
        ],
        compiler_params=pltpu.CompilerParams(
            collective_id=0, has_side_effects=True, vmem_limit_bytes=67043328
        ),
    )(mirror, surface, forward.reshape(chips * parts, time), records)
    return jnp.einsum(
        "gskr,kt->gsrt", total, inverse.reshape(chips * parts, time),
        preferred_element_type=jnp.float32,
    ).astype(jnp.bfloat16)


def solution(mesh):
    return jax.shard_map(
        local,
        mesh=mesh,
        in_specs=(P("pair", "shot", None, None), P("shot", None), P()),
        out_specs=P("pair", "shot", None, None),
        check_vma=False,
    )
```

time: 79.8 us -> 74.8 us (0.937)
  the two profiles are of different devices: /device:TPU:20 before, /device:TPU:0 now
where the time goes in v2:
time: 74.8 us; the launch traced here: 74.6 us
  Pallas kernels  68.3 us (91%)
  matrix products  4.93 us (7%)
  local copies, waits for them, and re-layouts  1.21 us (2%)
    pallas_call x1, Pallas kernels, local(): pl.pallas_call(functools.partial(kernel, chips, cores), out_shape=jax.Sha...  68.3 us
    dot_general x1, matrix products, local(): jnp.einsum('gskr,kt->gsrt', total, inverse.reshape(chips * parts, time),...  4.93 us

profile of v2, /device:TPU:0, one launch (start us, length us, event | category | flops | bytes accessed | tf_op | source)
XLA Modules:
  0.0 74.6 jit_solution(14166271179949581016)
XLA Ops:
  0.0 0.1 fusion.6
  0.2 0.6 copy.6
  0.8 0.6 copy.5
  1.4 68.3 %shard_map.37 = bf16[2,24,32,384]{3,2,1,0:T(8,128)(2,1)} custom-call(s32[4]{0:T(128)} %mirror_ref.1, f32[1,384]{1,0:T(1,128)} %surface_ref.1, bf16[32,128]{1,0:T(8,128)(2,1)} %bitcast.9, bf16[2,24,384,128]{3,2,1,0:T(8,128)(2,1)} %records_ref.1), custom_call_target="tpu_custom_call" | custom-call | tf_op jit(solution)/shard_map/pallas_call | solution.py:227
  69.7 4.9 %convolution_convert_fusion = bf16[2,24,384,128]{3,2,1,0:T(8,128)(2,1)} fusion(bf16[2,24,32,384]{3,2,1,0:T(8,128)(2,1)} %shard_map.37, bf16[32,128,1,1]{1,0,3,2:T(8,128)(2,1)} %bitcast.8), kind=kOutput, calls=%fused_computation | convolution fusion | flops 153354240 | bytes 5906432 | tf_op jit(solution)/shard_map/gskr,kt->gsrt/dot_general | solution.py:260
  (2 shorter events, 0.0 us)

commit v3 on v2

v3 whole, which is shorter than its diff:
```python
import functools
import math

import jax
import jax.numpy as jnp
from jax import lax
from jax.experimental import pallas as pl
from jax.experimental.pallas import tpu as pltpu
from jax.sharding import PartitionSpec as P

ORDERS = 2
MESH = pl.DeviceIdType.MESH


def make_tables(freqs, time):
    row = lax.broadcasted_iota(jnp.int32, (2 * freqs, time), 0)
    product = (row // 2 + 1) * lax.broadcasted_iota(jnp.int32, (2 * freqs, time), 1) % time
    phase = product.astype(jnp.float32) * (2.0 * math.pi / time)
    wave = jnp.where(row % 2 == 0, jnp.cos(phase), -jnp.sin(phase))
    forward = (wave * math.sqrt(2.0 / time)).astype(jnp.bfloat16)
    inverse = (wave / math.sqrt(freqs)).astype(jnp.bfloat16)
    return (forward, inverse)


def kernel(
    chips, cores, mirror_hbm, surface_hbm, forward_ref, records_ref, out_ref,
    traces, stage, send, held, left, block, first, totals, back, surface_ref, mirror_ref,
    small_sems, load_sems, own_sems, send_sems, recv_sems, pass_sems, pass_recv_sems,
    back_send_sems, back_recv_sems,
):
    me = lax.axis_index("shot")
    core = lax.axis_index("pair")
    groups, parts, shots, width = send.shape[1:]
    freqs = parts // 2
    loads = load_sems.shape[1]
    chunk = shots // loads
    half = chips // 2
    quarter = chips // 4
    across = jnp.where(me < half, 1, 0)

    def chip(step):
        return lax.rem(me + step, chips)

    def peer(step):
        return lax.rem(core + step, cores)

    def turned(index, size):
        inner = lax.rem(index + me, size) + size * (index // size)
        return lax.rem(across * size + inner, 2 * size)

    def middle(index):
        return quarter + turned(index, quarter)

    def outer(index):
        place = turned(index, quarter)
        return jnp.where(place < quarter, place, place + half)

    def load(group, index):
        some = pl.ds(index * chunk, chunk)
        return pltpu.make_async_copy(
            records_ref.at[group, some], traces.at[group, some], load_sems.at[group, index]
        )

    for group in range(groups):
        for index in range(loads):
            load(group, index).start()
    surface_copy = pltpu.make_async_copy(surface_hbm, surface_ref, small_sems.at[0])
    mirror_copy = pltpu.make_async_copy(mirror_hbm, mirror_ref, small_sems.at[1])
    surface_copy.start()
    mirror_copy.start()

    barrier = pltpu.get_barrier_semaphore()

    @pl.loop(1, chips)
    def _(step):
        pl.semaphore_signal(barrier, inc=1, device_id=(core, chip(step)), device_id_type=MESH)

    for step in range(1, cores):
        pl.semaphore_signal(barrier, inc=1, device_id=(peer(step), me), device_id_type=MESH)

    def spread(source, target, group):
        return pltpu.make_async_remote_copy(
            src_ref=send.at[target, group],
            dst_ref=held.at[core, group, :, source],
            send_sem=send_sems.at[group, target],
            recv_sem=recv_sems.at[group, source],
            device_id=(core, target),
            device_id_type=MESH,
        )

    def hand_on(source, other, group):
        return pltpu.make_async_remote_copy(
            src_ref=held.at[core, group, :, source],
            dst_ref=held.at[core, group, :, source],
            send_sem=pass_sems.at[other, group, source],
            recv_sem=pass_recv_sems.at[other, group, source],
            device_id=(peer(other), me),
            device_id_type=MESH,
        )

    def keep(group):
        return pltpu.make_async_copy(
            send.at[me, group], held.at[core, group, :, me], own_sems.at[group]
        )

    def send_back(source, target, group):
        return pltpu.make_async_remote_copy(
            src_ref=totals.at[target, group],
            dst_ref=back.at[source, group],
            send_sem=back_send_sems.at[group, target],
            recv_sem=back_recv_sems.at[group, source],
            device_id=(core, target),
            device_id_type=MESH,
        )

    def spread_half(target_of, group):
        @pl.loop(0, half)
        def _(index):
            target = target_of(index)

            @pl.when(target != me)
            def _():
                spread(me, target, group).start()

    for group in range(groups):
        for index in range(loads):
            load(group, index).wait()
            for shot in range(index * chunk, (index + 1) * chunk):
                stage[shot] = lax.dot_general(
                    forward_ref[...], traces[group, shot], (((1,), (1,)), ((), ())),
                    preferred_element_type=jnp.float32,
                )
        for row in range(chips * parts):
            send[row // parts, group, row % parts] = stage[:, row, :].astype(jnp.bfloat16)
        if group == 0:
            pl.semaphore_wait(barrier, chips + cores - 2)
        spread_half(middle, group)
        keep(group).start()
    for group in range(groups):
        spread_half(outer, group)

    surface_copy.wait()
    mirror_copy.wait()
    for group in range(groups):
        keep(group).wait()
        for other in range(1, cores):
            hand_on(me, other, group).start()

        @pl.loop(1, chips)
        def _(step):
            source = chip(step)
            spread(source, source, group).wait_recv()
            for other in range(1, cores):
                hand_on(source, other, group).start()

    @pl.loop(0, chips)
    def _(source):
        for group in range(groups):
            for other in range(1, cores):
                hand_on(source, other, group).wait()

    def matrix(slot, group, part):
        value = held[slot, group, part].astype(jnp.float32)
        return value.reshape(chips * shots, width)

    tall = chips * shots
    span = 16 if chips % 16 == 0 else chips
    tile = width if width % 256 == 0 else 2 * width
    for group in range(groups):
        mate = mirror_ref[core * groups + group]
        mate_slot = mate // groups
        mate_group = lax.rem(mate, groups)
        for freq in range(freqs):
            scale = -surface_ref[pl.ds(freq, 1), :] / math.sqrt(2.0 * width)
            mate_re = matrix(mate_slot, mate_group, 2 * freq)
            mate_im = matrix(mate_slot, mate_group, 2 * freq + 1)
            block[:tall, :width] = mate_re.astype(jnp.bfloat16)
            block[tall:, width:] = mate_re.astype(jnp.bfloat16)
            block[:tall, width:] = mate_im.astype(jnp.bfloat16)
            block[tall:, :width] = (-mate_im).astype(jnp.bfloat16)
            for part in range(2):
                columns = slice(part * width, (part + 1) * width)
                value = matrix(core, group, 2 * freq + part)
                left[:, columns] = (value * scale).astype(jnp.bfloat16)
            for order in range(ORDERS):
                for top in range(0, chips, span):
                    band = slice(top * shots, (top + span) * shots)
                    pieces = []
                    for start in range(0, 2 * width, tile):
                        piece = jnp.dot(
                            left[band, :], block[:, start : start + tile],
                            preferred_element_type=jnp.float32,
                        )
                        if order > 0:
                            piece = piece + first[band, start : start + tile]
                        if order + 1 < ORDERS:
                            first[band, start : start + tile] = piece
                            pieces.append(piece)
                        else:
                            for low in range(start, start + tile, width):
                                total = piece[:, low - start : low - start + width]
                                totals[top : top + span, group, 2 * freq + low // width] = (
                                    total.reshape(span, shots, width).astype(jnp.bfloat16)
                                )
                    if order + 1 < ORDERS:
                        product = jnp.concatenate(pieces, axis=1) if len(pieces) > 1 else pieces[0]
                        wide = jnp.concatenate([scale, scale], axis=1)
                        left[band, :] = (product * wide).astype(jnp.bfloat16)

        @pl.loop(0, chips)
        def _(index):
            target = turned(index, half)

            @pl.when(target != me)
            def _():
                send_back(me, target, group).start()

        for part in range(parts):
            own = totals[me, group, part].astype(jnp.float32)
            back[me, group, part] = own.astype(jnp.bfloat16)

    @pl.loop(1, chips)
    def _(step):
        for group in range(groups):
            spread(me, chip(step), group).wait_send()

    for group in range(groups):

        @pl.loop(0, chips)
        def _(source):
            @pl.when(source != me)
            def _():
                send_back(source, source, group).wait()

            for part in range(parts):
                value = back[source, group, part].astype(jnp.float32)
                stage[:, pl.ds(source * parts + part, 1), :] = value[:, None, :]

        out_ref[group] = stage[...].astype(jnp.bfloat16)


def local(records, surface, mirror):
    chips = lax.axis_size("shot")
    cores = lax.axis_size("pair")
    groups, shots, receivers, time = records.shape
    freqs = surface.shape[0]
    parts = 2 * freqs
    forward, inverse = make_tables(freqs * chips, time)
    tall = chips * shots
    loads = 4 if shots % 4 == 0 else 1
    block_shape = (chips, groups, parts, shots, receivers)
    dma = pltpu.SemaphoreType.DMA
    total_shape = (groups, shots, chips * parts, receivers)
    scratch = [
        (records.shape, jnp.bfloat16),
        ((shots, chips * parts, receivers), jnp.float32),
        (block_shape, jnp.bfloat16),
        ((cores, groups, parts, chips, shots, receivers), jnp.bfloat16),
        ((tall, 2 * receivers), jnp.bfloat16),
        ((2 * tall, 2 * receivers), jnp.bfloat16),
        ((tall, 2 * receivers), jnp.float32),
        (block_shape, jnp.bfloat16),
        (block_shape, jnp.bfloat16),
    ]
    held_bytes = sum(math.prod(shape) * jnp.dtype(kind).itemsize for shape, kind in scratch)
    roomy = held_bytes < 24 * 1024 * 1024
    grant = held_bytes + 8 * 1024 * 1024 if roomy else 67043328
    out_shape = pltpu.VMEM if roomy else jax.ShapeDtypeStruct
    total = pl.pallas_call(
        functools.partial(kernel, chips, cores),
        out_shape=out_shape(total_shape, jnp.bfloat16),
        in_specs=[
            pl.BlockSpec(memory_space=pltpu.HBM),
            pl.BlockSpec(memory_space=pltpu.HBM),
            pl.BlockSpec(memory_space=pltpu.VMEM),
            pl.BlockSpec(memory_space=pltpu.HBM),
        ],
        out_specs=pl.BlockSpec(memory_space=pltpu.VMEM),
        scratch_shapes=[
            *(pltpu.VMEM(shape, kind) for shape, kind in scratch),
            pltpu.VMEM(surface.shape, jnp.float32),
            pltpu.SMEM(mirror.shape, jnp.int32),
            dma((2,)),
            dma((groups, loads)),
            dma((groups,)),
            dma((groups, chips)),
            dma((groups, chips)),
            dma((cores, groups, chips)),
            dma((cores, groups, chips)),
            dma((groups, chips)),
            dma((groups, chips)),
        ],
        compiler_params=pltpu.CompilerParams(
            collective_id=0, has_side_effects=True, vmem_limit_bytes=grant
        ),
    )(
        pltpu.with_memory_space_constraint(mirror, pltpu.HBM),
        pltpu.with_memory_space_constraint(surface, pltpu.HBM),
        forward,
        pltpu.with_memory_space_constraint(records, pltpu.HBM),
    )
    return jnp.einsum("gskr,kt->gsrt", total, inverse, preferred_element_type=jnp.float32).astype(
        jnp.bfloat16
    )


def solution(mesh):
    return jax.shard_map(
        local,
        mesh=mesh,
        in_specs=(P("pair", "shot", None, None), P("shot", None), P()),
        out_specs=P("pair", "shot", None, None),
        check_vma=False,
    )
```

time: 74.8 us -> 66.1 us (0.88)
  Pallas kernels: 68.3 us -> 62.5 us
  matrix products: 4.93 us -> 3.3 us
  local copies, waits for them, and re-layouts: 1.21 us -> 0 us
    pallas_call x1, Pallas kernels: 68.3 us -> 62.5 us  [local(): pl.pallas_call(functools.partial(kernel, chips, cores), out_shape=out_sha...]
    dot_general x1, matrix products: 4.93 us -> 3.3 us  [local(): jnp.einsum('gskr,kt->gsrt', total, inverse, preferred_element_type=jnp.fl...]
    convert_element_type x2 -> x0, local copies, waits for them, and re-layouts: 1.21 us -> none  [the longest x1 0.6 us: make_tables(): (jnp.stack([cosine, -sine], axis=1) * math.sqrt(2.0 / time)).astype(jnp.b...]
where the time goes in v3:
time: 66.1 us; the launch traced here: 66 us
  Pallas kernels  62.5 us (95%)
  matrix products  3.3 us (5%)
    pallas_call x1, Pallas kernels, local(): pl.pallas_call(functools.partial(kernel, chips, cores), out_shape=out_sha...  62.5 us
    dot_general x1, matrix products, local(): jnp.einsum('gskr,kt->gsrt', total, inverse, preferred_element_type=jnp.fl...  3.3 us

profile of v3, /device:TPU:0, one launch (start us, length us, event | category | flops | bytes accessed | tf_op | source)
XLA Modules:
  0.0 66.0 jit_solution(17688634695731716402)
XLA Ops:
  0.0 0.2 multiply_convert_fusion.1.forward_ref
  0.2 62.5 %shard_map.37 = bf16[2,24,32,384]{3,2,1,0:T(8,128)(2,1)S(1)} custom-call(s32[4]{0:T(128)} %mirror_hbm.1, f32[1,384]{1,0:T(1,128)} %surface_hbm.1, bf16[32,128]{1,0:T(8,128)(2,1)S(1)} %multiply_convert_fusion.1.forward_ref, bf16[2,24,384,128]{3,2,1,0:T(8,128)(2,1)} %records_ref.1), custom_call_target="tpu_custom_call" | custom-call | tf_op jit(solution)/shard_map/pallas_call | solution.py:269
  62.7 3.3 %convolution_convert_fusion = bf16[2,24,384,128]{3,2,1,0:T(8,128)(2,1)} fusion(bf16[2,24,32,384]{3,2,1,0:T(8,128)(2,1)S(1)} %shard_map.37, s32[32]{0:T(128)S(1)} %get-tuple-element.7, s32[32]{0:T(128)S(1)} %get-tuple-element.9, s32[32]{0:T(128)S(1)} %get-tuple-element.8, s32[32]{0:T(128)S(1)} %get-tuple-element.10, pred[32]{0:T(512)(128)(4,1)S(1)} %get-tuple-element.5, ...), kind=kOutput, calls=%fused_computation | convolution fusion | flops 153444352 | bytes 5898816 | tf_op jit(solution)/shard_map/gskr,kt->gsrt/dot_general | solution.py:302
  (3 shorter events, 0.0 us)

commit v4 on v3

--- a/solution.py
+++ b/solution.py
@@ -36,7 +36,7 @@
     chunk = shots // loads
     half = chips // 2
     quarter = chips // 4
-    across = jnp.where(me < half, 1, 0)
+    across = jnp.where(me < half, 0, 1)
 
     def chip(step):
         return lax.rem(me + step, chips)

time: 66.1 us -> 64.4 us (0.974); the launches traced: 66 us -> 63.6 us
  Pallas kernels: 62.5 us -> 60.1 us
    pallas_call x1, Pallas kernels: 62.5 us -> 60.1 us  [local(): pl.pallas_call(functools.partial(kernel, chips, cores), out_shape=out_sha...]
where the time goes in v4:
time: 64.4 us; the launch traced here: 63.6 us
  Pallas kernels  60.1 us (93%)
  matrix products  3.31 us (5%)
    pallas_call x1, Pallas kernels, local(): pl.pallas_call(functools.partial(kernel, chips, cores), out_shape=out_sha...  60.1 us
    dot_general x1, matrix products, local(): jnp.einsum('gskr,kt->gsrt', total, inverse, preferred_element_type=jnp.fl...  3.31 us

profile of v4, /device:TPU:0, one launch (start us, length us, event | category | flops | bytes accessed | tf_op | source)
XLA Modules:
  0.0 63.6 jit_solution(8475660496860334424)
XLA Ops:
  0.0 0.2 multiply_convert_fusion.1.forward_ref
  0.2 60.1 %shard_map.37 = bf16[2,24,32,384]{3,2,1,0:T(8,128)(2,1)S(1)} custom-call(s32[4]{0:T(128)} %mirror_hbm.1, f32[1,384]{1,0:T(1,128)} %surface_hbm.1, bf16[32,128]{1,0:T(8,128)(2,1)S(1)} %multiply_convert_fusion.1.forward_ref, bf16[2,24,384,128]{3,2,1,0:T(8,128)(2,1)} %records_ref.1), custom_call_target="tpu_custom_call" | custom-call | tf_op jit(solution)/shard_map/pallas_call | solution.py:269
  60.3 3.3 %convolution_convert_fusion = bf16[2,24,384,128]{3,2,1,0:T(8,128)(2,1)} fusion(bf16[2,24,32,384]{3,2,1,0:T(8,128)(2,1)S(1)} %shard_map.37, s32[32]{0:T(128)S(1)} %get-tuple-element.7, s32[32]{0:T(128)S(1)} %get-tuple-element.9, s32[32]{0:T(128)S(1)} %get-tuple-element.8, s32[32]{0:T(128)S(1)} %get-tuple-element.10, pred[32]{0:T(512)(128)(4,1)S(1)} %get-tuple-element.5, ...), kind=kOutput, calls=%fused_computation | convolution fusion | flops 153444352 | bytes 5898816 | tf_op jit(solution)/shard_map/gskr,kt->gsrt/dot_general | solution.py:302
  (3 shorter events, 0.0 us)

commit v5 on v4

--- a/solution.py
+++ b/solution.py
@@ -146,12 +146,15 @@
         for other in range(1, cores):
             hand_on(me, other, group).start()
 
-        @pl.loop(1, chips)
-        def _(step):
-            source = chip(step)
-            spread(source, source, group).wait_recv()
-            for other in range(1, cores):
-                hand_on(source, other, group).start()
+        @pl.loop(0, chips)
+        def _(index):
+            source = turned(index, half)
+
+            @pl.when(source != me)
+            def _():
+                spread(source, source, group).wait_recv()
+                for other in range(1, cores):
+                    hand_on(source, other, group).start()
 
     @pl.loop(0, chips)
     def _(source):
@@ -227,7 +230,9 @@
     for group in range(groups):
 
         @pl.loop(0, chips)
-        def _(source):
+        def _(index):
+            source = turned(index, half)
+
             @pl.when(source != me)
             def _():
                 send_back(source, source, group).wait()

time: 64.4 us -> 64.5 us (level)
  no operation moved by 1% of the time
where the time goes in v5:
time: 64.5 us; the launch traced here: 63.7 us
  Pallas kernels  60.2 us (93%)
  matrix products  3.31 us (5%)
    pallas_call x1, Pallas kernels, local(): pl.pallas_call(functools.partial(kernel, chips, cores), out_shape=out_sha...  60.2 us
    dot_general x1, matrix products, local(): jnp.einsum('gskr,kt->gsrt', total, inverse, preferred_element_type=jnp.fl...  3.31 us

profile of v5, /device:TPU:0, one launch (start us, length us, event | category | flops | bytes accessed | tf_op | source)
XLA Modules:
  0.0 63.7 jit_solution(4690675615272250592)
XLA Ops:
  0.0 0.2 multiply_convert_fusion.1.forward_ref
  0.2 60.2 %shard_map.37 = bf16[2,24,32,384]{3,2,1,0:T(8,128)(2,1)S(1)} custom-call(s32[4]{0:T(128)} %mirror_hbm.1, f32[1,384]{1,0:T(1,128)} %surface_hbm.1, bf16[32,128]{1,0:T(8,128)(2,1)S(1)} %multiply_convert_fusion.1.forward_ref, bf16[2,24,384,128]{3,2,1,0:T(8,128)(2,1)} %records_ref.1), custom_call_target="tpu_custom_call" | custom-call | tf_op jit(solution)/shard_map/pallas_call | solution.py:274
  60.4 3.3 %convolution_convert_fusion = bf16[2,24,384,128]{3,2,1,0:T(8,128)(2,1)} fusion(bf16[2,24,32,384]{3,2,1,0:T(8,128)(2,1)S(1)} %shard_map.37, s32[32]{0:T(128)S(1)} %get-tuple-element.7, s32[32]{0:T(128)S(1)} %get-tuple-element.9, s32[32]{0:T(128)S(1)} %get-tuple-element.8, s32[32]{0:T(128)S(1)} %get-tuple-element.10, pred[32]{0:T(512)(128)(4,1)S(1)} %get-tuple-element.5, ...), kind=kOutput, calls=%fused_computation | convolution fusion | flops 153444352 | bytes 5898816 | tf_op jit(solution)/shard_map/gskr,kt->gsrt/dot_general | solution.py:307
  (3 shorter events, 0.0 us)
